TPU v7x, 32 devices: a whole 2x2x4 slice. The times are simulated.
32 devices in a mesh: row: 4 (over z), col: 4 (over y, x), feat: 2 (over core).
Axes of the slice: x: 2, y: 2, z: 4, core: 2. Of those that a mesh axis runs over, the one named last changes fastest.
Arguments:
- tile_values: bfloat16 [4, 4, 80, 128, 128], P('row', 'col')
- tile_rows: int32 [4, 4, 80], P('row', 'col'), may hold values from 0 to 15, as said below
- tile_cols: int32 [4, 4, 80], P('row', 'col'), may hold values from 0 to 15
- tile_mask: int32 [4, 4, 80], P('row', 'col'), may hold values from 0 to 1, as said below
- degree_caps: int32 [8192], P(('row', 'col')), may hold values from 1 to 32, as said below
- clip_groups: int32 [8192], P(('row', 'col')), may hold values from 0 to 7
- clip_bounds: float32 [8], replicated, may hold values from 51.2 to 256
- features: bfloat16 [8192, 256], P('col', 'feat')
- weight: bfloat16 [256, 256], replicated, may hold values from -0.375 to 0.375
- out_grad: bfloat16 [8192, 256], P(('row', 'col'), 'feat')
- dp_noise: float32 [256, 256], P(None, 'feat'), may hold values from -6 to 6
Outputs:
- out_feat: bfloat16 [8192, 256], P(('row', 'col'), 'feat')
- grad_weight: float32 [256, 256], P(None, 'feat')
- grad_input: bfloat16 [8192, 256], P('col', 'feat')
Inputs may be any that keep to these rules, and one draw needn't show every extreme that they name: `tile_rows`: each tile slot of one pair of row and col indices names a distinct pair of block row and block column. `tile_mask`: at most all 80 slots of one pair of row and col indices are live; in every draw some pair has all of them live. degree_caps[i] is the number of nonzero entries in row i of A, raised to 1 where it is 0 and capped at 32.
All inputs are finite; a program needn't handle non-finite values.
Results may differ from a plain program's by a relative error of at most 0.006.
Values may be sent and summed in bfloat16 or wider, within the bound.
A program may use at most 128 MiB of HBM per device.

v0:
```python
import math
import jax
import jax.numpy as jnp
from jax import lax
from jax.sharding import PartitionSpec as P


def slot_products(tile_vals, take_ids, source, flipped):
    contraction = "kji,kjf->kif" if flipped else "kij,kjf->kif"
    slot_total = tile_vals.shape[0]
    picked = jnp.take(source, take_ids, axis=0)
    products = jnp.einsum(contraction, tile_vals, picked, preferred_element_type=jnp.float32)
    return (products, jnp.arange(slot_total, dtype=jnp.int32))


def block_sums(products, put_ids, live_slots, block_count):
    wanted = jnp.arange(block_count, dtype=jnp.int32)
    selector = ((put_ids[:, None] == wanted[None, :]) & live_slots[:, None]).astype(jnp.float32)
    return jnp.einsum("kb,kif->bif", selector, products, precision=lax.Precision.HIGHEST)


def per_device(
    tile_values,
    tile_rows,
    tile_cols,
    tile_mask,
    degree_caps,
    clip_groups,
    clip_bounds,
    features,
    weight,
    out_grad,
    dp_noise,
):
    tile_vals = tile_values[0, 0]
    row_ids = tile_rows[0, 0]
    col_ids = tile_cols[0, 0]
    tile_live = tile_mask[0, 0]
    block_size = tile_vals.shape[1]
    half_width = features.shape[1]
    node_count = out_grad.shape[0]
    col_devices = lax.axis_size("col")
    row_devices = lax.axis_size("row")
    row_blocks = node_count * col_devices // block_size
    col_blocks = features.shape[0] // block_size
    grad_scale = 1.0 / math.sqrt(node_count * col_devices * row_devices)
    source = features.reshape(col_blocks, block_size, half_width)
    products, order = slot_products(tile_vals, col_ids, source, False)
    put_rows = jnp.take(row_ids, order)
    live_rows = jnp.take(tile_live, order) == 1
    partial_value = block_sums(products, put_rows, live_rows, row_blocks)
    partial_value = partial_value.reshape(row_blocks * block_size, half_width)
    summed = lax.psum_scatter(partial_value, "col", scatter_dimension=0, tiled=True)
    node_scale = lax.rsqrt(degree_caps.astype(jnp.float32))[:, None]
    agg_half = (summed * node_scale).astype(jnp.bfloat16)
    aggregate = lax.all_gather(agg_half, "feat", axis=1, tiled=True)
    feat_idx = lax.axis_index("feat")
    weight_cols = lax.dynamic_slice_in_dim(weight, feat_idx * half_width, half_width, 1)
    weight_rows = lax.dynamic_slice_in_dim(weight, feat_idx * half_width, half_width, 0)
    pre_act = jnp.dot(aggregate, weight_cols, preferred_element_type=jnp.float32)
    out_feat = jax.nn.silu(pre_act).astype(jnp.bfloat16)
    gate_sig = jax.nn.sigmoid(pre_act)
    grad_pre = (
        out_grad.astype(jnp.float32) * gate_sig * (1.0 + pre_act * (1.0 - gate_sig))
    ).astype(jnp.bfloat16)
    grad_full = lax.all_gather(grad_pre, "feat", axis=1, tiled=True)
    agg_sq = jnp.sum(jnp.square(aggregate.astype(jnp.float32)), axis=1)
    grad_sq = jnp.sum(jnp.square(grad_full.astype(jnp.float32)), axis=1)
    group_hits = (
        clip_groups[:, None] == jnp.arange(clip_bounds.shape[0], dtype=jnp.int32)[None, :]
    ).astype(jnp.float32)
    bounds = jnp.sum(group_hits * clip_bounds[None, :], axis=1)
    factor = jnp.minimum(1.0, bounds / (jnp.sqrt(agg_sq + 1e-06) * jnp.sqrt(grad_sq + 1e-06)))
    clipped = (factor[:, None] * grad_pre.astype(jnp.float32)).astype(jnp.bfloat16)
    local_grad = lax.dot_general(
        aggregate, clipped, (((0,), (0,)), ((), ())), preferred_element_type=jnp.float32
    )
    grad_weight = lax.psum(local_grad, ("row", "col")) * grad_scale + dp_noise
    back_prod = lax.dot_general(
        grad_full, weight_rows, (((1,), (1,)), ((), ())), preferred_element_type=jnp.float32
    )
    grad_agg = (back_prod * node_scale).astype(jnp.bfloat16)
    range_grads = lax.all_gather(grad_agg, "col", axis=0, tiled=True)
    grad_source = range_grads.reshape(row_blocks, block_size, half_width)
    back_products, back_order = slot_products(tile_vals, row_ids, grad_source, True)
    put_cols = jnp.take(col_ids, back_order)
    live_cols = jnp.take(tile_live, back_order) == 1
    input_part = block_sums(back_products, put_cols, live_cols, col_blocks)
    input_part = input_part.reshape(col_blocks * block_size, half_width)
    grad_input = lax.psum(input_part, "row").astype(jnp.bfloat16)
    return (out_feat, grad_weight, grad_input)


def solution(mesh):
    placed = (
        P("row", "col", None, None, None),
        P("row", "col", None),
        P("row", "col", None),
        P("row", "col", None),
        P(("row", "col")),
        P(("row", "col")),
        P(),
        P("col", "feat"),
        P(),
        P(("row", "col"), "feat"),
        P(None, "feat"),
    )
    return jax.shard_map(
        per_device,
        mesh=mesh,
        in_specs=placed,
        out_specs=(P(("row", "col"), "feat"), P(None, "feat"), P("col", "feat")),
        check_vma=False,
    )
```

profile of v0, /device:TPU:0, one launch (start us, length us, event | category | flops | bytes accessed | tf_op | source)
XLA Modules:
  0.0 184.9 jit_solution(5821199909000592426)
XLA Ops:
  7.2 0.0 copy-start
  7.2 0.0 copy-start.3
  7.2 0.0 reduce-scatter.2.cloned.1.call-start
  7.2 0.9 compare_and_fusion.1
  8.1 0.7 compare_select_fusion.1
  8.8 1.6 gather_fusion.1
  10.4 1.6 gather_fusion
  12.0 0.0 copy-done.3
  12.0 2.5 %gather_fusion.2 = bf16[80,128,128]{2,1,0:T(8,128)(2,1)} fusion(bf16[16,128,128]{2,1,0:T(8,128)(2,1)S(1)} %bitcast.41, s32[1024]{0:T(1024)S(1)} %pad_clamp_fusion.1), kind=kCustom, calls=%fused_computation.1.clone | custom fusion | bytes 5243200 | tf_op jit(solution)/shard_map/jit(_take)/gather | solution.py:11
  14.6 0.0 copy-done
  14.6 6.2 %fusion.8 = f32[80,128,128]{1,2,0:T(8,128)} fusion(bf16[1,1,80,128,128]{4,3,2,1,0:T(8,128)(2,1)S(1)} %copy-done, bf16[80,128,128]{2,1,0:T(8,128)(2,1)} %gather_fusion.2, pred[80]{0:T(512)(128)(4,1)S(1)} %compare_and_fusion.1), kind=kOutput, calls=%fused_computation.13 | convolution fusion | flops 336855040 | bytes 10485840 | tf_op jit(solution)/shard_map/kij,kjf->kif/dot_general | solution.py:12
  20.7 6.4 %copy.21 = f32[80,128,128]{2,0,1:T(8,128)} copy(f32[80,128,128]{1,2,0:T(8,128)} %fusion.8) | data formatting | bytes 10485760 | tf_op jit(solution)/shard_map/kij,kjf->kif/dot_general | solution.py:12
  27.1 4.3 %fusion.28 = f32[16,128,128]{2,0,1:T(8,128)S(1)} fusion(f32[80,128,128]{2,0,1:T(8,128)} %copy.21, s32[80]{0:T(128)S(1)} %broadcast_select_fusion.1, pred[80]{0:T(512)(128)(4,1)S(1)} %select_compare_fusion), kind=kOutput, calls=%fused_computation.38 | convolution fusion | flops 251660800 | bytes 6291856 | tf_op jit(solution)/shard_map/kb,kif->bif/dot_general | solution.py:19
  31.5 0.0 copy-start.1
  31.5 0.0 copy-start.2
  31.5 0.0 copy-start.6
  31.5 0.0 copy-start.8
  31.5 0.0 copy-start.7
  31.5 0.0 copy-start.5
  31.5 0.0 copy-start.9
  31.5 1.3 copy.22
  32.8 0.0 reduce-scatter.2.cloned.1.call-update
  32.9 0.0 all-reduce.3.cloned.1.call-start
  32.9 0.0 copy-done.1
  32.9 1.2 gather_fusion.3
  34.2 0.0 copy-done.2
  34.2 0.0 copy-done.6
  34.2 0.1 select_reduce_fusion
  34.3 29.1 %reduce-scatter.2.cloned.1.call-done = f32[512,128]{1,0:T(8,128)} async-done(((f32[2048,128]{1,0:T(8,128)}), f32[512,128]{1,0:T(8,128)}) %reduce-scatter.2.cloned.1.call-update) | async-done | bytes 262160 | tf_op jit(solution)/shard_map/reduce_scatter | solution.py:53
  63.4 1.1 multiply_convert_fusion.3
  64.5 2.0 %all_gather.9 = bf16[512,256]{1,0:T(8,128)(2,1)S(1)} all-gather(bf16[512,128]{1,0:T(8,128)(2,1)S(1)} %multiply_convert_fusion.3), channel_id=1, replica_groups=mesh['row'=4,'col'=4,'feat'=2] {'feat'}, dimensions={1}, use_global_device_ids=true | all-gather | bytes 393216 | tf_op jit(solution)/shard_map/all_gather | solution.py:56
  66.5 0.1 multiply_reduce_fusion.1
  66.7 1.0 multiply_convert_fusion.1
  67.7 2.0 %all_gather.10 = bf16[512,256]{1,0:T(8,128)(2,1)S(1)} all-gather(bf16[512,128]{1,0:T(8,128)(2,1)S(1)} %get-tuple-element.5), channel_id=1, replica_groups=mesh['row'=4,'col'=4,'feat'=2] {'feat'}, dimensions={1}, use_global_device_ids=true | all-gather | bytes 393216 | tf_op jit(solution)/shard_map/all_gather | solution.py:66
  69.6 0.1 multiply_reduce_fusion
  69.8 0.2 fusion.20
  70.0 1.0 fusion.21
  71.1 0.0 all-reduce.3.cloned.1.call-update
  71.1 10.2 %all_gather.11 = bf16[2048,128]{1,0:T(8,128)(2,1)S(1)} all-gather(bf16[512,128]{1,0:T(8,128)(2,1)S(1)} %fusion.20), channel_id=1, replica_groups=mesh['row'=4,'col'=4,'feat'=2] {'col'}, dimensions={0}, use_global_device_ids=true | all-gather | bytes 655360 | tf_op jit(solution)/shard_map/all_gather | solution.py:83
  81.3 2.5 %gather_fusion.4 = bf16[80,128,128]{2,1,0:T(8,128)(2,1)} fusion(bf16[16,128,128]{2,1,0:T(8,128)(2,1)S(1)} %bitcast.40, s32[1024]{0:T(1024)S(1)} %pad_clamp_fusion), kind=kCustom, calls=%fused_computation.4.clone | custom fusion | bytes 5243200 | tf_op jit(solution)/shard_map/jit(_take)/gather | solution.py:11
  83.8 5.2 %fusion.13 = f32[80,128,128]{1,2,0:T(8,128)} fusion(bf16[1,1,80,128,128]{4,3,2,1,0:T(8,128)(2,1)S(1)} %copy-done, bf16[80,128,128]{2,1,0:T(8,128)(2,1)} %gather_fusion.4, pred[80]{0:T(512)(128)(4,1)S(1)} %compare_and_fusion), kind=kOutput, calls=%fused_computation.14 | convolution fusion | flops 336855040 | bytes 10485840 | tf_op jit(solution)/shard_map/kji,kjf->kif/dot_general | solution.py:12
  89.0 6.4 %copy.24 = f32[80,128,128]{2,0,1:T(8,128)} copy(f32[80,128,128]{1,2,0:T(8,128)} %fusion.13) | data formatting | bytes 10485760 | tf_op jit(solution)/shard_map/kji,kjf->kif/dot_general | solution.py:12
  95.4 4.3 %fusion.32 = f32[16,128,128]{2,0,1:T(8,128)S(1)} fusion(f32[80,128,128]{2,0,1:T(8,128)} %copy.24, s32[80]{0:T(128)S(1)} %broadcast_select_fusion, pred[80]{0:T(512)(128)(4,1)S(1)} %select_compare_fusion), kind=kOutput, calls=%fused_computation.41 | convolution fusion | flops 251660800 | bytes 6291856 | tf_op jit(solution)/shard_map/kb,kif->bif/dot_general | solution.py:19
  99.8 0.0 copy-start.4
  99.8 1.3 copy.25
  101.1 44.6 %all-reduce.4 = bf16[2048,128]{1,0:T(8,128)(2,1)} all-reduce(f32[2048,128]{1,0:T(8,128)} %bitcast.43), channel_id=1, replica_groups=mesh['row'=4,'col'=4,'feat'=2] {'row'}, use_global_device_ids=true, to_apply=%region_5.8 | all-reduce | flops 262144 | bytes 1572864 | tf_op jit(solution)/shard_map/psum | solution.py:90
  145.7 30.7 %all-reduce.3.cloned.1.call-done = f32[256,128]{1,0:T(8,128)} async-done(((f32[256,128]{1,0:T(8,128)}), f32[256,128]{1,0:T(8,128)}) %all-reduce.3.cloned.1.call-update) | async-done | bytes 131088 | tf_op jit(solution)/shard_map/psum | solution.py:78
  176.5 1.6 multiply_add_fusion
  (16 shorter events, 0.1 us)
Async XLA Ops:
  7.2 7.4 %copy-start = (bf16[1,1,80,128,128]{4,3,2,1,0:T(8,128)(2,1)S(1)}, bf16[1,1,80,128,128]{4,3,2,1,0:T(8,128)(2,1)}, u32[]{:S(2)}) copy-start(bf16[1,1,80,128,128]{4,3,2,1,0:T(8,128)(2,1)} %param.15) | copy-start | bytes 7864324
  7.2 4.8 %copy-start.3 = (bf16[2048,128]{1,0:T(8,128)(2,1)S(1)}, bf16[2048,128]{1,0:T(8,128)(2,1)}, u32[]{:S(2)}) copy-start(bf16[2048,128]{1,0:T(8,128)(2,1)} %param.22) | copy-start | bytes 1572868
  7.2 56.3 %reduce-scatter.2.cloned.1.call-start = ((), (), s32[]{:S(2)}) async-start(), calls=%async_computation.1 | async-start | bytes 1310720 | tf_op jit(solution)/shard_map/reduce_scatter | solution.py:53
  31.5 1.5 copy-start.1
  31.5 2.7 %copy-start.2 = (s32[1,1,80]{2,1,0:T(1,128)S(1)}, s32[1,1,80]{2,1,0:T(1,128)}, u32[]{:S(2)}) copy-start(s32[1,1,80]{2,1,0:T(1,128)} %param.16) | copy-start | bytes 964
  31.5 2.7 %copy-start.6 = (s32[512]{0:T(512)S(1)}, s32[512]{0:T(512)}, u32[]{:S(2)}) copy-start(s32[512]{0:T(512)} %param.20) | copy-start | bytes 6148
  31.5 2.7 %copy-start.8 = (f32[8]{0:T(128)S(1)}, f32[8]{0:T(128)}, u32[]{:S(2)}) copy-start(f32[8]{0:T(128)} %param.21) | copy-start | bytes 100
  31.5 2.8 %copy-start.7 = (s32[512]{0:T(512)S(1)}, s32[512]{0:T(512)}, u32[]{:S(2)}) copy-start(s32[512]{0:T(512)} %param.19) | copy-start | bytes 6148
  31.5 35.2 %copy-start.5 = (bf16[256,256]{1,0:T(8,128)(2,1)S(1)}, bf16[256,256]{1,0:T(8,128)(2,1)}, u32[]{:S(2)}) copy-start(bf16[256,256]{1,0:T(8,128)(2,1)} %param.23) | copy-start | bytes 393220
  31.5 35.2 %copy-start.9 = (bf16[512,128]{1,0:T(8,128)(2,1)S(1)}, bf16[512,128]{1,0:T(8,128)(2,1)}, u32[]{:S(2)}) copy-start(bf16[512,128]{1,0:T(8,128)(2,1)} %param.24) | copy-start | bytes 393220
  32.9 143.6 %all-reduce.3.cloned.1.call-start = ((), (), s32[]{:S(2)}) async-start(), calls=%async_computation.2 | async-start | bytes 262144 | tf_op jit(solution)/shard_map/psum | solution.py:78
  99.8 76.7 %copy-start.4 = (f32[256,128]{1,0:T(8,128)S(1)}, f32[256,128]{1,0:T(8,128)}, u32[]{:S(2)}) copy-start(f32[256,128]{1,0:T(8,128)} %param.25) | copy-start | bytes 393220
Sparse Core Ops, SparseCore 0:
  33.0 30.4 reduce-scatter.1
  71.2 105.2 all-reduce.2
where the time goes:
time: 185 us
  waiting for transfers between devices  59.9 us (32%)
  blocking collectives  58.8 us (32%)
  local copies, waits for them, and re-layouts  24.9 us (13%)
  matrix products  22.3 us (12%)
  between operations  14.3 us (8%)
  other arithmetic  4.65 us (3%)
    psum x1, blocking collectives, per_device(): grad_input = lax.psum(input_part, 'row').astype(jnp.bfloat16)  44.6 us
    psum x1, waiting for transfers between devices, per_device(): grad_weight = lax.psum(local_grad, ('row', 'col')) * grad_scale + dp_noise  30.7 us
    reduce_scatter x1, waiting for transfers between devices, per_device(): lax.psum_scatter(partial_value, 'col', scatter_dimension=0, tiled=True)  29.1 us
    dot_general x2, local copies, waits for them, and re-layouts, slot_products(): jnp.einsum(contraction, tile_vals, picked, preferred_element_type=jnp.flo...  12.8 us
    dot_general x2, matrix products, slot_products(): jnp.einsum(contraction, tile_vals, picked, preferred_element_type=jnp.flo...  11.4 us
    all_gather x1, blocking collectives, per_device(): range_grads = lax.all_gather(grad_agg, 'col', axis=0, tiled=True)  10.2 us
    dot_general x2, matrix products, block_sums(): jnp.einsum('kb,kif->bif', selector, products, precision=lax.Precision.HIG...  8.69 us
    gather x2, local copies, waits for them, and re-layouts, slot_products(): picked = jnp.take(source, take_ids, axis=0)  5.08 us
  transfers between devices with their start and end apart: 2, of which 2 were waited for; matrix products, arithmetic and copies ran while one was open for 11% of the time, Pallas kernels for 0%

commit v1 on v0

--- a/solution.py
+++ b/solution.py
@@ -3,6 +3,28 @@
 import jax.numpy as jnp
 from jax import lax
 from jax.sharding import PartitionSpec as P
+from jax.lax import axis_index, axis_size, ppermute
+
+
+def recover_wall(across, x_in):
+    state_next, odd, small = (axis_size(across), axis_index(across), x_in.shape[0])
+    cards = [(dev, (dev + 1) % state_next) for dev in range(state_next)]
+    seen = [(dev, (dev - 1) % state_next) for dev in range(state_next)]
+    s_next = jnp.zeros((*x_in.shape[:0], state_next * small, *x_in.shape[1:]), x_in.dtype)
+    s_next = lax.dynamic_update_slice_in_dim(s_next, x_in, odd * small, axis=0)
+    seen_now = formed = x_in
+    w1 = state_next // 2
+    for dev_j in tuple(range(1, w1 + 1)):
+        seen_now = ppermute(seen_now, axis_name=across, perm=cards)
+        s_next = lax.dynamic_update_slice_in_dim(
+            s_next, seen_now, (odd - dev_j) % state_next * small, axis=0
+        )
+        if dev_j < state_next - w1:
+            formed = ppermute(formed, perm=seen, axis_name=across)
+            s_next = lax.dynamic_update_slice_in_dim(
+                s_next, formed, (odd + dev_j) % state_next * small, axis=0
+            )
+    return s_next
 
 
 def slot_products(tile_vals, take_ids, source, flipped):
@@ -80,7 +102,7 @@
         grad_full, weight_rows, (((1,), (1,)), ((), ())), preferred_element_type=jnp.float32
     )
     grad_agg = (back_prod * node_scale).astype(jnp.bfloat16)
-    range_grads = lax.all_gather(grad_agg, "col", axis=0, tiled=True)
+    range_grads = recover_wall("col", x_in=grad_agg)
     grad_source = range_grads.reshape(row_blocks, block_size, half_width)
     back_products, back_order = slot_products(tile_vals, row_ids, grad_source, True)
     put_cols = jnp.take(col_ids, back_order)

time: 185 us -> 253 us (1.37)
  waiting for transfers between devices: 59.9 us -> 133 us
  blocking collectives: 58.8 us -> 46.6 us
  starting transfers between devices: 0.08 us -> 4.44 us
    psum x1, waiting for transfers between devices: 30.7 us -> 99.5 us  [per_device(): grad_weight = lax.psum(local_grad, ('row', 'col')) * grad_scale + dp_noise]
    all_gather x1 -> x0, blocking collectives: 10.2 us -> none  [per_device(): range_grads = lax.all_gather(grad_agg, 'col', axis=0, tiled=True)]
    ppermute x0 -> x3, waiting for transfers between devices: none -> 4.37 us  [the longest x2 4.37 us: recover_wall(): seen_now = ppermute(seen_now, axis_name=across, perm=cards)]
    ppermute x0 -> x3, starting transfers between devices: none -> 4.36 us  [the longest x2 2.84 us: recover_wall(): seen_now = ppermute(seen_now, axis_name=across, perm=cards)]
  transfers between devices with their start and end apart: 2 -> 5, of which waited for: 2 -> 3; matrix products, arithmetic and copies ran while one was open for 11% -> 2% of each run, Pallas kernels for 0% -> 0%
where the time goes in v1:
time: 253 us; the launch traced here: 252 us
  waiting for transfers between devices  133 us (53%)
  blocking collectives  46.6 us (18%)
  local copies, waits for them, and re-layouts  25.3 us (10%)
  matrix products  23.7 us (9%)
  between operations  14.3 us (6%)
  other arithmetic  5.1 us (2%)
  starting transfers between devices  4.44 us (2%)
    psum x1, waiting for transfers between devices, per_device(): grad_weight = lax.psum(local_grad, ('row', 'col')) * grad_scale + dp_noise  99.5 us
    psum x1, blocking collectives, per_device(): grad_input = lax.psum(input_part, 'row').astype(jnp.bfloat16)  42.6 us
    reduce_scatter x1, waiting for transfers between devices, per_device(): lax.psum_scatter(partial_value, 'col', scatter_dimension=0, tiled=True)  28.6 us
    dot_general x2, local copies, waits for them, and re-layouts, slot_products(): jnp.einsum(contraction, tile_vals, picked, preferred_element_type=jnp.flo...  12.8 us
    dot_general x2, matrix products, slot_products(): jnp.einsum(contraction, tile_vals, picked, preferred_element_type=jnp.flo...  11.3 us
    dot_general x2, matrix products, block_sums(): jnp.einsum('kb,kif->bif', selector, products, precision=lax.Precision.HIG...  8.69 us
    gather x2, local copies, waits for them, and re-layouts, slot_products(): picked = jnp.take(source, take_ids, axis=0)  6.1 us
  transfers between devices with their start and end apart: 5, of which 3 were waited for; matrix products, arithmetic and copies ran while one was open for 2% of the time, Pallas kernels for 0%

profile of v1, /device:TPU:0, one launch (start us, length us, event | category | flops | bytes accessed | tf_op | source)
XLA Modules:
  0.0 252.1 jit_solution(12405316663045354448)
XLA Ops:
  7.2 0.0 copy-start
  7.2 0.0 reduce-scatter.2.cloned.1.call-start
  7.2 0.8 compare_select_fusion.1
  8.0 0.7 compare_and_fusion
  8.7 3.6 %gather_fusion.2 = bf16[80,128,128]{2,1,0:T(8,128)(2,1)} fusion(bf16[16,128,128]{2,1,0:T(8,128)(2,1)} %bitcast.41, s32[1024]{0:T(1024)S(1)} %pad_clamp_fusion.1), kind=kCustom, calls=%fused_computation.1.clone | custom fusion | bytes 5243200 | tf_op jit(solution)/shard_map/jit(_take)/gather | solution.py:33
  12.3 6.1 %fusion.8 = f32[80,128,128]{1,2,0:T(8,128)} fusion(bf16[1,1,80,128,128]{4,3,2,1,0:T(8,128)(2,1)S(1)} %copy-done, bf16[80,128,128]{2,1,0:T(8,128)(2,1)} %gather_fusion.2, pred[80]{0:T(512)(128)(4,1)S(1)} %get-tuple-element.10), kind=kOutput, calls=%fused_computation.13 | convolution fusion | flops 336855040 | bytes 10485840 | tf_op jit(solution)/shard_map/kij,kjf->kif/dot_general | solution.py:34
  18.4 6.4 %copy.21 = f32[80,128,128]{2,0,1:T(8,128)} copy(f32[80,128,128]{1,2,0:T(8,128)} %fusion.8) | data formatting | bytes 10485760 | tf_op jit(solution)/shard_map/kij,kjf->kif/dot_general | solution.py:34
  24.8 0.0 copy-done.2
  24.9 1.2 gather_fusion
  26.1 1.2 gather_fusion.1
  27.4 4.3 %fusion.28 = f32[16,128,128]{2,0,1:T(8,128)S(1)} fusion(f32[80,128,128]{2,0,1:T(8,128)} %copy.21, s32[80]{0:T(128)S(1)} %broadcast_select_fusion.1, pred[80]{0:T(512)(128)(4,1)S(1)} %select_compare_fusion), kind=kOutput, calls=%fused_computation.38 | convolution fusion | flops 251660800 | bytes 6291856 | tf_op jit(solution)/shard_map/kb,kif->bif/dot_general | solution.py:41
  31.7 0.0 copy-start.1
  31.7 0.0 copy-start.6
  31.7 0.0 copy-start.8
  31.7 0.0 copy-start.7
  31.8 0.0 copy-start.5
  31.8 0.0 copy-start.10
  31.8 1.3 copy.22
  33.1 0.0 reduce-scatter.2.cloned.1.call-update
  33.1 0.0 all-reduce.3.cloned.1.call-start
  33.2 1.2 gather_fusion.3
  34.5 0.1 select_reduce_fusion
  34.6 0.5 broadcast_select_fusion
  35.1 28.6 %reduce-scatter.2.cloned.1.call-done = f32[512,128]{1,0:T(8,128)} async-done(((f32[2048,128]{1,0:T(8,128)}), f32[512,128]{1,0:T(8,128)}) %reduce-scatter.2.cloned.1.call-update) | async-done | bytes 262160 | tf_op jit(solution)/shard_map/reduce_scatter | solution.py:75
  63.8 1.1 multiply_convert_fusion.3
  64.8 2.0 all_gather.6
  66.8 0.1 multiply_reduce_fusion.1
  67.0 1.0 multiply_convert_fusion.1
  68.0 2.0 all_gather.7
  69.9 0.1 multiply_reduce_fusion
  70.1 1.0 fusion.21
  71.1 0.0 all-reduce.3.cloned.1.call-update
  71.2 0.1 broadcast_in_dim.17
  71.2 1.8 constant_dynamic-update-slice_fusion.3
  73.0 1.4 collective-permute-start
  74.4 1.5 collective-permute-start.1
  75.9 99.5 %all-reduce.3.cloned.1.call-done = f32[256,128]{1,0:T(8,128)} async-done(((f32[256,128]{1,0:T(8,128)}), f32[256,128]{1,0:T(8,128)}) %all-reduce.3.cloned.1.call-update) | async-done | bytes 131088 | tf_op jit(solution)/shard_map/psum | solution.py:100
  175.4 1.6 multiply_add_fusion
  177.0 0.0 collective-permute-done
  177.0 1.4 collective-permute-start.2
  178.5 0.0 collective-permute-done.1
  178.5 4.4 %collective-permute-done.2 = bf16[512,128]{1,0:T(8,128)(2,1)S(1)} collective-permute-done((bf16[512,128]{1,0:T(8,128)(2,1)S(1)}, bf16[512,128]{1,0:T(8,128)(2,1)S(1)}, u32[]{:S(2)}, u32[]{:S(2)}) %collective-permute-start.2) | collective-permute-done | bytes 131104 | tf_op jit(solution)/shard_map/ppermute | solution.py:18
  182.9 2.5 %gather_fusion.4 = bf16[80,128,128]{2,1,0:T(8,128)(2,1)} fusion(bf16[16,128,128]{2,1,0:T(8,128)(2,1)S(1)} %bitcast.40, s32[1024]{0:T(1024)S(1)} %pad_clamp_fusion), kind=kCustom, calls=%fused_computation.4.clone | custom fusion | bytes 5243200 | tf_op jit(solution)/shard_map/jit(_take)/gather | solution.py:33
  185.4 5.2 %fusion.13 = f32[80,128,128]{1,2,0:T(8,128)} fusion(bf16[1,1,80,128,128]{4,3,2,1,0:T(8,128)(2,1)S(1)} %copy-done, bf16[80,128,128]{2,1,0:T(8,128)(2,1)} %gather_fusion.4, pred[80]{0:T(512)(128)(4,1)S(1)} %get-tuple-element.9), kind=kOutput, calls=%fused_computation.14 | convolution fusion | flops 336855040 | bytes 10485840 | tf_op jit(solution)/shard_map/kji,kjf->kif/dot_general | solution.py:34
  190.6 6.4 %copy.24 = f32[80,128,128]{2,0,1:T(8,128)} copy(f32[80,128,128]{1,2,0:T(8,128)} %fusion.13) | data formatting | bytes 10485760 | tf_op jit(solution)/shard_map/kji,kjf->kif/dot_general | solution.py:34
  197.0 4.3 %fusion.32 = f32[16,128,128]{2,0,1:T(8,128)S(1)} fusion(f32[80,128,128]{2,0,1:T(8,128)} %copy.24, s32[80]{0:T(128)S(1)} %copy-done.9, pred[80]{0:T(512)(128)(4,1)S(1)} %select_compare_fusion), kind=kOutput, calls=%fused_computation.41 | convolution fusion | flops 251660800 | bytes 6291856 | tf_op jit(solution)/shard_map/kb,kif->bif/dot_general | solution.py:41
  201.3 1.3 copy.25
  202.6 42.6 %all-reduce.4 = bf16[2048,128]{1,0:T(8,128)(2,1)} all-reduce(f32[2048,128]{1,0:T(8,128)} %bitcast.43), channel_id=1, replica_groups=mesh['row'=4,'col'=4,'feat'=2] {'row'}, use_global_device_ids=true, to_apply=%region_5.8 | all-reduce | flops 262144 | bytes 1572864 | tf_op jit(solution)/shard_map/psum | solution.py:112
  (26 shorter events, 0.1 us)
Async XLA Ops:
  7.2 5.1 %copy-start = (bf16[1,1,80,128,128]{4,3,2,1,0:T(8,128)(2,1)S(1)}, bf16[1,1,80,128,128]{4,3,2,1,0:T(8,128)(2,1)}, u32[]{:S(2)}) copy-start(bf16[1,1,80,128,128]{4,3,2,1,0:T(8,128)(2,1)} %param.15) | copy-start | bytes 7864324
  7.2 56.6 %reduce-scatter.2.cloned.1.call-start = ((), (), s32[]{:S(2)}) async-start(), calls=%async_computation.1 | async-start | bytes 1310720 | tf_op jit(solution)/shard_map/reduce_scatter | solution.py:75
  18.4 6.4 %copy-start.2 = (s32[1,1,80]{2,1,0:T(1,128)S(1)}, s32[1,1,80]{2,1,0:T(1,128)}, u32[]{:S(2)}) copy-start(s32[1,1,80]{2,1,0:T(1,128)} %param.16) | copy-start | bytes 964
  18.4 7.7 %copy-start.3 = (s32[1,1,80]{2,1,0:T(1,128)S(1)}, s32[1,1,80]{2,1,0:T(1,128)}, u32[]{:S(2)}) copy-start(s32[1,1,80]{2,1,0:T(1,128)} %param.18) | copy-start | bytes 964
  31.7 1.5 copy-start.1
  31.7 2.8 %copy-start.6 = (s32[512]{0:T(512)S(1)}, s32[512]{0:T(512)}, u32[]{:S(2)}) copy-start(s32[512]{0:T(512)} %param.20) | copy-start | bytes 6148
  31.7 2.8 %copy-start.8 = (f32[8]{0:T(128)S(1)}, f32[8]{0:T(128)}, u32[]{:S(2)}) copy-start(f32[8]{0:T(128)} %param.21) | copy-start | bytes 100
  31.7 3.4 %copy-start.7 = (s32[512]{0:T(512)S(1)}, s32[512]{0:T(512)}, u32[]{:S(2)}) copy-start(s32[512]{0:T(512)} %param.19) | copy-start | bytes 6148
  31.8 35.2 %copy-start.5 = (bf16[256,256]{1,0:T(8,128)(2,1)S(1)}, bf16[256,256]{1,0:T(8,128)(2,1)}, u32[]{:S(2)}) copy-start(bf16[256,256]{1,0:T(8,128)(2,1)} %param.23) | copy-start | bytes 393220
  31.8 35.2 %copy-start.10 = (bf16[512,128]{1,0:T(8,128)(2,1)S(1)}, bf16[512,128]{1,0:T(8,128)(2,1)}, u32[]{:S(2)}) copy-start(bf16[512,128]{1,0:T(8,128)(2,1)} %param.24) | copy-start | bytes 393220
  33.1 142.3 %all-reduce.3.cloned.1.call-start = ((), (), s32[]{:S(2)}) async-start(), calls=%async_computation.2 | async-start | bytes 262144 | tf_op jit(solution)/shard_map/psum | solution.py:100
  35.1 140.3 %copy-start.4 = (f32[256,128]{1,0:T(8,128)S(1)}, f32[256,128]{1,0:T(8,128)}, u32[]{:S(2)}) copy-start(f32[256,128]{1,0:T(8,128)} %param.25) | copy-start | bytes 393220
  73.0 104.0 %collective-permute-start = (bf16[512,128]{1,0:T(8,128)(2,1)}, bf16[512,128]{1,0:T(8,128)(2,1)S(1)}, u32[]{:S(2)}, u32[]{:S(2)}) collective-permute-start(bf16[512,128]{1,0:T(8,128)(2,1)} %get-tuple-element.8), channel_id=1, source_target_pairs={{0,2},{2,4},{4,6},{6,0},{1,3},{3,5},{5,7},{7,1},{8,10},{10,12},{12... | collective-permute-start | bytes 393224 | tf_op jit(solution)/shard_map/ppermute | solution.py:18
  74.4 104.1 %collective-permute-start.1 = (bf16[512,128]{1,0:T(8,128)(2,1)}, bf16[512,128]{1,0:T(8,128)(2,1)S(1)}, u32[]{:S(2)}, u32[]{:S(2)}) collective-permute-start(bf16[512,128]{1,0:T(8,128)(2,1)} %get-tuple-element.8), channel_id=1, source_target_pairs={{0,6},{2,0},{4,2},{6,4},{1,7},{3,1},{5,3},{7,5},{8,14},{10,8},{12,... | collective-permute-start | bytes 393224 | tf_op jit(solution)/shard_map/ppermute | solution.py:23
  177.0 5.9 %collective-permute-start.2 = (bf16[512,128]{1,0:T(8,128)(2,1)S(1)}, bf16[512,128]{1,0:T(8,128)(2,1)S(1)}, u32[]{:S(2)}, u32[]{:S(2)}) collective-permute-start(bf16[512,128]{1,0:T(8,128)(2,1)S(1)} %collective-permute-done), channel_id=1, source_target_pairs={{0,2},{2,4},{4,6},{6,0},{1,3},{3,5},{5,7},{7,1},{8,10},{10,12},{12... | collective-permute-start | bytes 393224 | tf_op jit(solution)/shard_map/ppermute | solution.py:18
  190.6 6.4 %copy-start.9 = (s32[80]{0:T(128)S(1)}, s32[80]{0:T(128)}, u32[]{:S(2)}) copy-start(s32[80]{0:T(128)} %broadcast_select_fusion) | copy-start | bytes 964
Sparse Core Ops, SparseCore 0:
  33.2 30.4 reduce-scatter.1
  71.3 104.1 all-reduce.2
